TPU v7x, 128 devices: a whole 4x4x4 slice. The times are simulated.
128 devices in a mesh: wide: 32 (over x, z, core), narrow: 4 (over y).
Axes of the slice: x: 4, y: 4, z: 4, core: 2. Of those that a mesh axis runs over, the one named last changes fastest.
Arguments:
- member: bfloat16 [2048, 8192], P('narrow', 'wide'), may hold values from 0.01 to 300, as said below
Outputs:
- transition: float32 [8192, 8192], P('wide', 'narrow')
- stationary: float32 [8192], P('wide')
Inputs may be any that keep to these rules, and one draw needn't show every extreme that they name: `member`: strictly positive weights.
All inputs are finite; a program needn't handle non-finite values.
Results may differ from a plain program's by a relative error of at most 0.0003.
Values may be sent and summed in bfloat16 or wider, within the bound.
No kernel may reach another device: no remote copies, remote signals or barrier semaphores. Data moves between devices by JAX's collectives and lax.ppermute only.
A program may use at most 128 MiB of HBM per device.

v0:
```python
import jax
import jax.numpy as jnp
from jax import lax
from jax.sharding import PartitionSpec as P

STATES = 8192
TAU = 64
ITERS = 3


def passed_along(block, axis, distance):
    devices = range(lax.axis_size(axis))
    route = [(i - distance, i) for i in devices if i - distance in devices]
    return lax.ppermute(block, axis, route)


def contract_frames(left, right):
    return lax.dot_general(
        left, right, (((0,), (0,)), ((), ())), preferred_element_type=jnp.float32
    )


def shards(member):
    rim = passed_along(member[:TAU], "narrow", -1)
    lagged = jnp.concatenate([member[TAU:], rim], axis=0)
    frame_part = jnp.sum(lagged, axis=1, dtype=jnp.float32)
    frame_totals = lax.psum(frame_part, "wide")
    visit_part = jnp.dot(frame_totals, member.astype(jnp.float32), precision=lax.Precision.HIGHEST)
    stacked = jnp.stack([member, lagged])
    piece = lax.all_gather(stacked, "wide", axis=2, tiled=True)
    partial_value = contract_frames(member, piece[1]) + contract_frames(lagged, piece[0])
    counts = lax.psum_scatter(partial_value, "narrow", scatter_dimension=1, tiled=True)
    row_now, visit_rows = lax.psum((jnp.sum(counts, axis=1), visit_part), "narrow")
    visit_all = lax.all_gather(visit_rows, "wide", axis=0, tiled=True)
    width_cols = counts.shape[1]
    col_start = lax.axis_index("narrow") * width_cols
    visit_cols = lax.dynamic_slice_in_dim(visit_all, col_start, width_cols)
    estimate = counts
    for step in range(ITERS):
        all_rows = lax.all_gather(row_now, "wide", axis=0, tiled=True)
        col_now = lax.dynamic_slice_in_dim(all_rows, col_start, width_cols)
        ratio_rows = visit_rows / row_now
        ratio_cols = visit_cols / col_now
        estimate = counts / (ratio_rows[:, None] + ratio_cols[None, :])
        row_now = lax.psum(jnp.sum(estimate, axis=1), "narrow")
    transition = STATES * estimate / row_now[:, None]
    grand = lax.psum(jnp.sum(row_now), "wide")
    stationary = STATES * row_now / grand
    return (transition, stationary)


def solution(mesh):
    return jax.shard_map(
        shards,
        mesh=mesh,
        in_specs=(P("narrow", "wide"),),
        out_specs=(P("wide", "narrow"), P("wide")),
        check_vma=False,
    )
```

profile of v0, /device:TPU:1, one launch (start us, length us, event | category | flops | bytes accessed | tf_op | source)
XLA Modules:
  0.0 404.0 jit_solution(7120169739386829088)
XLA Ops:
  7.2 0.0 all-gather.6.cloned.1.call-start
  7.2 0.8 slice.13
  8.0 1.3 collective-permute-start
  9.3 1.0 slice.12
  10.3 3.1 collective-permute-done
  13.3 1.8 pad_maximum_fusion
  15.2 0.0 reduce-scatter.2.cloned.1.call-start
  15.2 84.3 %all-gather.6.cloned.1.call-done = bf16[2,512,8192]{2,1,0:T(8,128)(2,1)} async-done(((bf16[2,512,256]{2,1,0:T(8,128)(2,1)}), bf16[2,512,8192]{2,1,0:T(8,128)(2,1)}) %all-gather.6.cloned.1.call-update) | async-done | bytes 16777232 | tf_op jit(solution)/shard_map/all_gather | solution.py:30
  99.5 5.8 %convolution_bitcast_fusion = f32[256,8192]{0,1:T(8,128)S(1)} fusion(bf16[512,256]{1,0:T(8,128)(2,1)S(1)} %copy-done.1, bf16[2,512,8192]{2,1,0:T(8,128)(2,1)} %all-gather.6.cloned.1.call-done), kind=kOutput, calls=%fused_computation | convolution fusion | flops 2147483648 | bytes 17039360 | tf_op jit(solution)/shard_map/dot_general | solution.py:18
  105.3 10.0 %convolution_add_fusion = f32[256,8192]{0,1:T(8,128)} fusion(f32[256,8192]{0,1:T(8,128)S(1)} %convolution_bitcast_fusion, bf16[2,512,8192]{2,1,0:T(8,128)(2,1)} %all-gather.6.cloned.1.call-done, bf16[64,256]{1,0:T(8,128)(2,1)S(1)} %collective-permute-done, bf16[448,256]{1,0:T(8,128)(2,1)S(1)} %slice.12), kind=kOutput, calls=%fused_computation.1 | convolution fusion | flops 2150105088 | bytes 25427968 | tf_op jit(solution)/shard_map/dot_general | solution.py:18
  115.2 0.0 reduce-scatter.2.cloned.1.call-update
  115.3 0.1 convert_reduce_fusion
  115.4 62.3 %psum.49 = f32[512]{0:T(512)S(1)} all-reduce(f32[512]{0:T(512)S(1)} %convert_reduce_fusion), channel_id=1, replica_groups=mesh['wide'=32,'narrow'=4] {'wide'}, use_global_device_ids=true, to_apply=%region_2.0 | all-reduce | flops 512 | bytes 4096 | tf_op jit(solution)/shard_map/psum | solution.py:27
  177.7 0.2 fusion.5
  177.9 17.7 %reduce-scatter.2.cloned.1.call-done = f32[256,2048]{0,1:T(8,128)} async-done(((f32[256,8192]{0,1:T(8,128)}), f32[256,2048]{0,1:T(8,128)}) %reduce-scatter.2.cloned.1.call-update) | async-done | bytes 2097168 | tf_op jit(solution)/shard_map/reduce_scatter | solution.py:32
  195.6 2.0 reduce_sum.55
  197.6 6.5 %all-reduce = (f32[256]{0:T(256)S(1)}, f32[256]{0:T(256)S(1)}) all-reduce(f32[256]{0:T(256)S(1)} %reduce_sum.55, f32[256]{0:T(256)S(1)} %bitcast.35), channel_id=1, replica_groups=mesh['wide'=32,'narrow'=4] {'narrow'}, use_global_device_ids=true, to_apply=%region_5.0 | all-reduce | flops 512 | bytes 4096 | tf_op jit(solution)/shard_map/psum | solution.py:33
  204.2 27.0 %all-gather = f32[32,1,256]{2,1,0:T(1,128)S(1)} all-gather(f32[1,1,256]{2,1,0:T(1,128)S(1)} %bitcast.31), channel_id=1, replica_groups=mesh['wide'=32,'narrow'=4] {'wide'}, dimensions={0}, use_global_device_ids=true | all-gather | bytes 33792 | tf_op jit(solution)/shard_map/all_gather | solution.py:34
  231.2 23.6 %all-gather.1 = f32[32,1,256]{2,1,0:T(1,128)S(1)} all-gather(f32[1,1,256]{2,1,0:T(1,128)S(1)} %bitcast.36), channel_id=1, replica_groups=mesh['wide'=32,'narrow'=4] {'wide'}, dimensions={0}, use_global_device_ids=true | all-gather | bytes 33792 | tf_op jit(solution)/shard_map/all_gather | solution.py:40
  254.8 0.4 fusion
  255.1 6.9 %psum.52 = f32[256]{0:T(256)S(1)} all-reduce(f32[256]{0:T(256)S(1)} %fusion), channel_id=1, replica_groups=mesh['wide'=32,'narrow'=4] {'narrow'}, use_global_device_ids=true, to_apply=%region_7.0 | all-reduce | flops 256 | bytes 2048 | tf_op jit(solution)/shard_map/psum | solution.py:45
  262.0 24.1 %all-gather.2 = f32[32,1,256]{2,1,0:T(1,128)S(1)} all-gather(f32[1,1,256]{2,1,0:T(1,128)S(1)} %bitcast.33), channel_id=1, replica_groups=mesh['wide'=32,'narrow'=4] {'wide'}, dimensions={0}, use_global_device_ids=true | all-gather | bytes 33792 | tf_op jit(solution)/shard_map/all_gather | solution.py:40
  286.1 0.4 fusion.1
  286.5 6.6 %psum.53 = f32[256]{0:T(256)S(1)} all-reduce(f32[256]{0:T(256)S(1)} %fusion.1), channel_id=1, replica_groups=mesh['wide'=32,'narrow'=4] {'narrow'}, use_global_device_ids=true, to_apply=%region_9.0 | all-reduce | flops 256 | bytes 2048 | tf_op jit(solution)/shard_map/psum | solution.py:45
  293.0 25.6 %all-gather.3 = f32[32,1,256]{2,1,0:T(1,128)S(1)} all-gather(f32[1,1,256]{2,1,0:T(1,128)S(1)} %bitcast.32), channel_id=1, replica_groups=mesh['wide'=32,'narrow'=4] {'wide'}, dimensions={0}, use_global_device_ids=true | all-gather | bytes 33792 | tf_op jit(solution)/shard_map/all_gather | solution.py:40
  318.6 0.4 fusion.2
  319.0 6.9 %psum.54 = f32[256]{0:T(256)S(1)} all-reduce(f32[256]{0:T(256)S(1)} %fusion.2), channel_id=1, replica_groups=mesh['wide'=32,'narrow'=4] {'narrow'}, use_global_device_ids=true, to_apply=%region_11.0 | all-reduce | flops 256 | bytes 2048 | tf_op jit(solution)/shard_map/psum | solution.py:45
  325.9 0.6 reduce_sum.59
  326.5 64.8 %psum.55 = f32[]{:T(128)} all-reduce(f32[]{:T(128)} %reduce_sum.59), channel_id=1, replica_groups=mesh['wide'=32,'narrow'=4] {'wide'}, use_global_device_ids=true, to_apply=%region_13.0 | all-reduce | flops 1 | bytes 8 | tf_op jit(solution)/shard_map/psum | solution.py:47
  391.3 1.2 multiply_divide_fusion.1
  392.5 1.8 multiply_divide_fusion
  394.3 2.9 copy.6
  (12 shorter events, 0.1 us)
Async XLA Ops:
  7.2 92.3 %copy-start.1 = (bf16[512,256]{1,0:T(8,128)(2,1)S(1)}, bf16[512,256]{1,0:T(8,128)(2,1)}, u32[]{:S(2)}) copy-start(bf16[512,256]{1,0:T(8,128)(2,1)} %param.1) | copy-start | bytes 786436
  7.2 92.3 %all-gather.6.cloned.1.call-start = ((), (), s32[]{:S(2)}) async-start(), calls=%async_computation.1 | async-start | bytes 17301504 | tf_op jit(solution)/shard_map/all_gather | solution.py:30
  8.0 5.3 %collective-permute-start = (bf16[64,256]{1,0:T(8,128)(2,1)S(1)}, bf16[64,256]{1,0:T(8,128)(2,1)S(1)}, u32[]{:S(2)}, u32[]{:S(2)}) collective-permute-start(bf16[64,256]{1,0:T(8,128)(2,1)S(1)} %slice.13), channel_id=1, source_target_pairs={{1,0},{2,1},{3,2},{5,4},{6,5},{7,6},{9,8},{10,9},{11,10},{13,12},{... | collective-permute-start | bytes 98312 | tf_op jit(solution)/shard_map/ppermute | solution.py:14
  15.2 180.4 %reduce-scatter.2.cloned.1.call-start = ((), (), s32[]{:S(2)}) async-start(), calls=%async_computation.2 | async-start | bytes 10485760 | tf_op jit(solution)/shard_map/reduce_scatter | solution.py:32
  195.6 59.2 %copy-start = (f32[256,2048]{0,1:T(8,128)S(1)}, f32[256,2048]{0,1:T(8,128)}, u32[]{:S(2)}) copy-start(f32[256,2048]{0,1:T(8,128)} %reduce-scatter.2.cloned.1.call-done) | copy-start | bytes 6291460
Sparse Core Ops, SparseCore 0:
  15.3 84.1 all-gather.5
  115.4 80.1 reduce-scatter.1
where the time goes:
time: 405 us; the launch traced here: 404 us
  blocking collectives  254 us (63%)
  waiting for transfers between devices  105 us (26%)
  matrix products  15.9 us (4%)
  between operations  14.1 us (3%)
  other arithmetic  8.7 us (2%)
  local copies, waits for them, and re-layouts  4.64 us (1%)
    all_gather x1, waiting for transfers between devices, shards(): piece = lax.all_gather(stacked, 'wide', axis=2, tiled=True)  84.3 us
    all_gather x3, blocking collectives, shards(): all_rows = lax.all_gather(row_now, 'wide', axis=0, tiled=True)  73.2 us
    psum x1, blocking collectives, shards(): grand = lax.psum(jnp.sum(row_now), 'wide')  64.8 us
    psum x1, blocking collectives, shards(): frame_totals = lax.psum(frame_part, 'wide')  62.3 us
    all_gather x1, blocking collectives, shards(): visit_all = lax.all_gather(visit_rows, 'wide', axis=0, tiled=True)  27 us
    psum x3, blocking collectives, shards(): row_now = lax.psum(jnp.sum(estimate, axis=1), 'narrow')  20.3 us
    reduce_scatter x1, waiting for transfers between devices, shards(): lax.psum_scatter(partial_value, 'narrow', scatter_dimension=1, tiled=True)  17.7 us
    dot_general x2, matrix products, contract_frames(): lax.dot_general(left, right, (((0,), (0,)), ((), ())), preferred_element_...  15.7 us
  transfers between devices with their start and end apart: 3, of which 3 were waited for; matrix products, arithmetic and copies ran while one was open for 0% of the time, Pallas kernels for 0%

commit v1 on v0

v1 whole, which is shorter than its diff:
```python
import jax
import jax.numpy as jnp
from jax import lax
from jax.experimental import pallas as pl
from jax.experimental.pallas import tpu as pltpu
from jax.sharding import Mesh, PartitionSpec as P

STATES = 8192
TAU = 64
ITERS = 3
FRAMES = 2048
WIDE = ("x", "z", "c")
ALL = ("x", "z", "c", "y")
BLOCK = 512
WIDTH = 256
COLS = 2048
GROUPS = COLS // WIDTH


def place(x, y, z, c):
    return ((x * 4 + z) * 2 + c) * 4 + y


def across():
    return [
        (place(x, y, z, c), place(y, x, z, c))
        for x in range(4) for y in range(4) for z in range(4) for c in range(2)
    ]


def along(k):
    return [(i, (i + k) % 4) for i in range(4)]


def to_all(values):
    sent = jnp.broadcast_to(values[None], (128,) + values.shape)
    got = lax.all_to_all(sent, ALL, 0, 0)
    return got.reshape((32, 4) + values.shape)


def multiply(rows_t, weights, piece):
    def kernel(rows_ref, weight_ref, piece_ref, sym_ref, col_ref, row_ref):
        g = pl.program_id(0)

        @pl.when(g == 0)
        def _():
            row_ref[...] = lax.dot_general(
                weight_ref[...], rows_ref[:, TAU:TAU + FRAMES],
                (((1,), (1,)), ((), ())), preferred_element_type=jnp.float32)

        acc = jnp.zeros((WIDTH, WIDTH), jnp.float32)
        col = jnp.zeros((16, WIDTH), jnp.float32)
        for q in range(4):
            block = piece_ref[q, 0]
            lo = q * BLOCK
            acc += jnp.dot(rows_ref[:, lo:lo + BLOCK], block, preferred_element_type=jnp.float32)
            acc += jnp.dot(rows_ref[:, lo + 2 * TAU:lo + 2 * TAU + BLOCK], block,
                           preferred_element_type=jnp.float32)
            col += jnp.dot(weight_ref[:, lo:lo + BLOCK], block, preferred_element_type=jnp.float32)
        sym_ref[...] = acc
        col_ref[...] = col

    return pl.pallas_call(
        kernel,
        grid=(GROUPS,),
        in_specs=[
            pl.BlockSpec((WIDTH, FRAMES + 2 * TAU), lambda g: (0, 0)),
            pl.BlockSpec((16, FRAMES), lambda g: (0, 0)),
            pl.BlockSpec((4, 1, BLOCK, WIDTH), lambda g: (0, g, 0, 0)),
        ],
        out_specs=[
            pl.BlockSpec((WIDTH, WIDTH), lambda g: (0, g)),
            pl.BlockSpec((16, WIDTH), lambda g: (0, g)),
            pl.BlockSpec((16, WIDTH), lambda g: (0, 0)),
        ],
        out_shape=[
            jax.ShapeDtypeStruct((WIDTH, COLS), jnp.float32),
            jax.ShapeDtypeStruct((16, COLS), jnp.float32),
            jax.ShapeDtypeStruct((16, WIDTH), jnp.float32),
        ],
    )(rows_t, weights, piece)


def three_parts(v):
    hi = v.astype(jnp.bfloat16)
    rest = v - hi.astype(jnp.float32)
    mid = rest.astype(jnp.bfloat16)
    lo = (rest - mid.astype(jnp.float32)).astype(jnp.bfloat16)
    return [hi, mid, lo]


def own_rows(member):
    y = lax.axis_index("y")
    later = [lax.ppermute(member, "y", along(-k)) for k in (1, 2, 3)]
    turned = jnp.concatenate([member] + later, axis=0).T
    rows = jnp.roll(turned, y * BLOCK, axis=1)
    return jnp.pad(rows, ((0, 0), (TAU, TAU)))


def shards(member):
    y = lax.axis_index("y")
    w = (lax.axis_index("x") * 4 + lax.axis_index("z")) * 2 + lax.axis_index("c")
    moved = lax.ppermute(member, ALL, across())
    piece = lax.all_gather(moved, WIDE, axis=0).reshape(4, GROUPS, BLOCK, WIDTH)
    rows_t = own_rows(member)
    part = jnp.sum(member, axis=1, dtype=jnp.float32)
    frame = jnp.sum(to_all(part), axis=0).reshape(FRAMES)
    up = jnp.pad(frame[TAU:], (0, TAU))
    down = jnp.pad(frame[:FRAMES - TAU], (TAU, 0))
    weights = jnp.stack(three_parts(up) + three_parts(down))
    weights = jnp.pad(weights, ((0, 10), (0, 0)))
    sym, col_sums, row_sums = multiply(rows_t, weights, piece)
    visit_rows = jnp.sum(row_sums[:3], axis=0)
    total_rows = jnp.sum(row_sums[:6], axis=0)
    visit_cols = jnp.sum(col_sums[:3], axis=0)
    total_cols = jnp.sum(col_sums[:6], axis=0)
    for step in range(ITERS):
        ratio_rows = visit_rows / total_rows
        ratio_cols = visit_cols / total_cols
        estimate = sym / (ratio_rows[:, None] + ratio_cols[None, :])
        totals = jnp.sum(to_all(jnp.sum(estimate, axis=1)), axis=1).reshape(STATES)
        total_rows = lax.dynamic_slice_in_dim(totals, w * WIDTH, WIDTH)
        total_cols = lax.dynamic_slice_in_dim(totals, y * COLS, COLS)
    transition = STATES * estimate / total_rows[:, None]
    stationary = STATES * total_rows / jnp.sum(totals)
    return (transition, stationary)


def solution(mesh):
    mesh = Mesh(mesh.devices.reshape(4, 4, 2, 4), ALL)
    return jax.shard_map(
        shards,
        mesh=mesh,
        in_specs=(P("y", WIDE),),
        out_specs=(P(WIDE, "y"), P(WIDE)),
        check_vma=False,
    )
```

time: 405 us -> 160 us (0.40)
  blocking collectives: 254 us -> 27.9 us
  waiting for transfers between devices: 105 us -> 45.3 us
  starting transfers between devices: 1.36 us -> 40.4 us
  matrix products: 15.9 us -> 0 us
  Pallas kernels: 0 us -> 11.3 us
  other arithmetic: 8.7 us -> 14 us
    psum x6 -> x0, blocking collectives: 154 us -> none  [the longest x1 64.8 us: shards(): grand = lax.psum(jnp.sum(row_now), 'wide')]
    all_gather x4 -> x0, blocking collectives: 100 us -> none  [the longest x3 73.2 us: shards(): all_rows = lax.all_gather(row_now, 'wide', axis=0, tiled=True)]
    all_gather x1, waiting for transfers between devices: 84.3 us -> 24.7 us  [shards(): piece = lax.all_gather(moved, WIDE, axis=0).reshape(4, GROUPS, BLOCK, WIDTH)]
    all_to_all x0 -> x2, starting transfers between devices: none -> 33.7 us  [to_all(): got = lax.all_to_all(sent, ALL, 0, 0)]
    all_to_all x0 -> x2, blocking collectives: none -> 27.9 us  [to_all(): got = lax.all_to_all(sent, ALL, 0, 0)]
    reduce_scatter x1 -> x0, waiting for transfers between devices: 17.7 us -> none  [shards(): lax.psum_scatter(partial_value, 'narrow', scatter_dimension=1, tiled=True)]
    all_to_all x0 -> x2, waiting for transfers between devices: none -> 17.3 us  [to_all(): got = lax.all_to_all(sent, ALL, 0, 0)]
    dot_general x3 -> x0, matrix products: 15.9 us -> none  [the longest x2 15.7 us: contract_frames(): lax.dot_general(left, right, (((0,), (0,)), ((), ())), preferred_element_...]
  transfers between devices with their start and end apart: 3 -> 7, of which waited for: 3 -> 4; matrix products, arithmetic and copies ran while one was open for 0% -> 4% of each run, Pallas kernels for 0% -> 0%
where the time goes in v1:
time: 160 us; the launch traced here: 159 us
  waiting for transfers between devices  45.3 us (28%)
  starting transfers between devices  40.4 us (25%)
  blocking collectives  27.9 us (17%)
  between operations  14.3 us (9%)
  other arithmetic  14 us (9%)
  Pallas kernels  11.3 us (7%)
  local copies, waits for them, and re-layouts  6.17 us (4%)
    all_to_all x2, starting transfers between devices, to_all(): got = lax.all_to_all(sent, ALL, 0, 0)  33.7 us
    all_to_all x2, blocking collectives, to_all(): got = lax.all_to_all(sent, ALL, 0, 0)  27.9 us
    all_gather x1, waiting for transfers between devices, shards(): piece = lax.all_gather(moved, WIDE, axis=0).reshape(4, GROUPS, BLOCK, WIDTH)  24.7 us
    all_to_all x2, waiting for transfers between devices, to_all(): got = lax.all_to_all(sent, ALL, 0, 0)  17.3 us
    pallas_call x1, Pallas kernels, multiply(): pl.pallas_call(kernel, grid=(GROUPS,), in_specs=[pl.BlockSpec((WIDTH, FRA...  11.3 us
    ppermute x3, starting transfers between devices, own_rows(): later = [lax.ppermute(member, 'y', along(-k)) for k in (1, 2, 3)]  5.01 us
    ppermute x3, waiting for transfers between devices, own_rows(): later = [lax.ppermute(member, 'y', along(-k)) for k in (1, 2, 3)]  3.27 us
  transfers between devices with their start and end apart: 7, of which 4 were waited for; matrix products, arithmetic and copies ran while one was open for 4% of the time, Pallas kernels for 0%

profile of v1, /device:TPU:1, one launch (start us, length us, event | category | flops | bytes accessed | tf_op | source)
XLA Modules:
  0.0 159.3 jit_solution(8142367247024891672)
XLA Ops:
  7.2 1.6 %collective-permute-start.3 = (bf16[512,256]{1,0:T(8,128)(2,1)}, bf16[512,256]{1,0:T(8,128)(2,1)S(1)}, u32[]{:S(2)}, u32[]{:S(2)}) collective-permute-start(bf16[512,256]{1,0:T(8,128)(2,1)} %param.1), channel_id=1, source_target_pairs={{0,0},{4,4},{8,8},{12,12},{16,16},{20,20},{24,24},{28,28},{1,32},{... | collective-permute-start | bytes 786440 | tf_op jit(solution)/shard_map/ppermute | solution.py:103
  8.8 0.7 copy-done.1
  9.5 1.1 convert_reduce_fusion
  10.6 0.8 broadcast_in_dim.8
  11.5 26.4 %all-to-all-start = ((f32[128,1,512]{2,1,0:T(1,128)}), f32[128,1,512]{2,1,0:T(1,128)S(1)}, u32[]{:S(2)}, u32[]{:S(2)}) async-start(f32[128,1,512]{2,1,0:T(1,128)} %broadcast_in_dim.8), calls=%async_computation | async-start | bytes 524288 | tf_op jit(solution)/shard_map/all_to_all | solution.py:37
  37.8 1.1 copy.23
  38.9 1.4 collective-permute-start.2
  40.4 2.5 %collective-permute-start.1 = (bf16[512,256]{0,1:T(8,128)(2,1)S(1)}, bf16[512,256]{0,1:T(8,128)(2,1)S(1)}, u32[]{:S(2)}, u32[]{:S(2)}) collective-permute-start(bf16[512,256]{0,1:T(8,128)(2,1)S(1)} %copy.23), channel_id=1, source_target_pairs={{0,2},{1,3},{2,0},{3,1},{4,6},{5,7},{6,4},{7,5},{8,10},{9,11},{10,... | collective-permute-start | bytes 786440 | tf_op jit(solution)/shard_map/ppermute | solution.py:94
  42.8 1.1 collective-permute-start
  44.0 7.2 %all-to-all-done = f32[128,1,512]{2,1,0:T(1,128)S(1)} async-done(((f32[128,1,512]{2,1,0:T(1,128)}), f32[128,1,512]{2,1,0:T(1,128)S(1)}, u32[]{:S(2)}, u32[]{:S(2)}) %all-to-all-start) | async-done | bytes 262176 | tf_op jit(solution)/shard_map/all_to_all | solution.py:37
  51.2 0.6 reduce.3
  52.4 0.6 pad.19.weight_ref
  53.0 3.3 %collective-permute-done.1 = bf16[512,256]{0,1:T(8,128)(2,1)S(1)} collective-permute-done((bf16[512,256]{0,1:T(8,128)(2,1)S(1)}, bf16[512,256]{0,1:T(8,128)(2,1)S(1)}, u32[]{:S(2)}, u32[]{:S(2)}) %collective-permute-start.1) | collective-permute-done | bytes 262176 | tf_op jit(solution)/shard_map/ppermute | solution.py:94
  56.4 0.6 fusion.2
  57.0 1.5 pad.16.rows_ref
  58.5 24.7 %all-gather.3.cloned.1.call-done = bf16[16384,256]{1,0:T(8,128)(2,1)} async-done(((bf16[512,256]{1,0:T(8,128)(2,1)}), bf16[16384,256]{1,0:T(8,128)(2,1)}) %all-gather.3.cloned.1.call-update) | async-done | bytes 8388624 | tf_op jit(solution)/shard_map/all_gather | solution.py:104
  83.2 11.3 %shard_map.30 = (f32[256,2048]{1,0:T(8,128)}, f32[16,2048]{1,0:T(8,128)}, f32[16,256]{1,0:T(8,128)}) custom-call(bf16[256,2176]{1,0:T(8,128)(2,1)} %pad.16.rows_ref, bf16[16,2048]{1,0:T(8,128)(2,1)} %pad.19.weight_ref, bf16[4,8,512,256]{3,2,1,0:T(8,128)(2,1)} %bitcast.11), custom_call_target="tpu_custom_call" | custom-call | tf_op jit(solution)/shard_map/pallas_call | solution.py:63
  94.5 0.9 slice_reduce_fusion.3
  95.4 0.7 slice_reduce_fusion.2
  96.1 0.9 slice_reduce_fusion.1
  97.0 0.9 slice_reduce_fusion
  97.9 2.0 %fusion = f32[256]{0:T(256)S(1)} fusion(f32[256,2048]{1,0:T(8,128)} %get-tuple-element.5, f32[2048]{0:T(1024)S(1)} %div.50, f32[256]{0:T(256)S(1)} %div.49), kind=kLoop, calls=%fused_computation.6 | loop fusion | flops 1572608 | bytes 2107392 | tf_op jit(solution)/shard_map/reduce_sum | solution.py:121
  99.9 0.7 broadcast_in_dim.9
  100.6 7.4 %all-to-all-start.1 = ((f32[128,1,256]{2,1,0:T(1,128)}), f32[128,1,256]{2,1,0:T(1,128)S(1)}, u32[]{:S(2)}, u32[]{:S(2)}) async-start(f32[128,1,256]{2,1,0:T(1,128)} %broadcast_in_dim.9), calls=%async_computation.1 | async-start | bytes 262144 | tf_op jit(solution)/shard_map/all_to_all | solution.py:37
  108.0 10.1 %all-to-all-done.1 = f32[128,1,256]{2,1,0:T(1,128)S(1)} async-done(((f32[128,1,256]{2,1,0:T(1,128)}), f32[128,1,256]{2,1,0:T(1,128)S(1)}, u32[]{:S(2)}, u32[]{:S(2)}) %all-to-all-start.1) | async-done | bytes 131104 | tf_op jit(solution)/shard_map/all_to_all | solution.py:37
  118.6 0.4 fusion.1
  119.1 14.0 %all_to_all.24 = f32[128,1,256]{2,1,0:T(1,128)S(1)} all-to-all(f32[128,1,256]{2,1,0:T(1,128)S(1)} %broadcast_in_dim.10), channel_id=1, replica_groups=mesh['x'=4,'z'=4,'c'=2,'y'=4] {'x','z','c','y'}, dimensions={0} | all-to-all | bytes 262144 | tf_op jit(solution)/shard_map/all_to_all | solution.py:37
  133.7 0.4 fusion.3
  134.2 13.9 %all_to_all.25 = f32[128,1,256]{2,1,0:T(1,128)S(1)} all-to-all(f32[128,1,256]{2,1,0:T(1,128)S(1)} %broadcast_in_dim.11), channel_id=1, replica_groups=mesh['x'=4,'z'=4,'c'=2,'y'=4] {'x','z','c','y'}, dimensions={0} | all-to-all | bytes 262144 | tf_op jit(solution)/shard_map/all_to_all | solution.py:37
  148.2 1.1 fusion.6
  149.4 1.3 multiply_divide_fusion.1
  150.7 1.8 %multiply_divide_fusion = f32[256,2048]{1,0:T(8,128)} fusion(f32[256]{0:T(256)S(1)} %get-tuple-element.11, f32[256,2048]{1,0:T(8,128)S(1)} %copy-done, f32[2048]{0:T(1024)S(1)} %dynamic-slice_divide_fusion, f32[256]{0:T(256)S(1)} %dynamic-slice_divide_fusion.2), kind=kLoop, calls=%fused_computation.2 | loop fusion | flops 2097152 | bytes 4204544 | tf_op jit(solution)/shard_map/div | solution.py:124
  (41 shorter events, 2.0 us)
Async XLA Ops:
  7.2 76.1 %all-gather.3.cloned.1.call-start = ((), (), s32[]{:S(2)}) async-start(), calls=%async_computation.4 | async-start | bytes 8650752 | tf_op jit(solution)/shard_map/all_gather | solution.py:104
  7.2 1.6 %collective-permute-start.3 = (bf16[512,256]{1,0:T(8,128)(2,1)}, bf16[512,256]{1,0:T(8,128)(2,1)S(1)}, u32[]{:S(2)}, u32[]{:S(2)}) collective-permute-start(bf16[512,256]{1,0:T(8,128)(2,1)} %param.1), channel_id=1, source_target_pairs={{0,0},{4,4},{8,8},{12,12},{16,16},{20,20},{24,24},{28,28},{1,32},{... | collective-permute-start | bytes 786440 | tf_op jit(solution)/shard_map/ppermute | solution.py:103
  8.8 0.7 copy-start.1
  11.5 39.7 %all-to-all-start = ((f32[128,1,512]{2,1,0:T(1,128)}), f32[128,1,512]{2,1,0:T(1,128)S(1)}, u32[]{:S(2)}, u32[]{:S(2)}) async-start(f32[128,1,512]{2,1,0:T(1,128)} %broadcast_in_dim.8), calls=%async_computation | async-start | bytes 524288 | tf_op jit(solution)/shard_map/all_to_all | solution.py:37
  38.9 14.0 %collective-permute-start.2 = (bf16[512,256]{0,1:T(8,128)(2,1)S(1)}, bf16[512,256]{0,1:T(8,128)(2,1)S(1)}, u32[]{:S(2)}, u32[]{:S(2)}) collective-permute-start(bf16[512,256]{0,1:T(8,128)(2,1)S(1)} %copy.23), channel_id=1, source_target_pairs={{0,1},{1,2},{2,3},{3,0},{4,5},{5,6},{6,7},{7,4},{8,9},{9,10},{10,1... | collective-permute-start | bytes 786440 | tf_op jit(solution)/shard_map/ppermute | solution.py:94
  40.4 15.9 %collective-permute-start.1 = (bf16[512,256]{0,1:T(8,128)(2,1)S(1)}, bf16[512,256]{0,1:T(8,128)(2,1)S(1)}, u32[]{:S(2)}, u32[]{:S(2)}) collective-permute-start(bf16[512,256]{0,1:T(8,128)(2,1)S(1)} %copy.23), channel_id=1, source_target_pairs={{0,2},{1,3},{2,0},{3,1},{4,6},{5,7},{6,4},{7,5},{8,10},{9,11},{10,... | collective-permute-start | bytes 786440 | tf_op jit(solution)/shard_map/ppermute | solution.py:94
  42.8 13.4 %collective-permute-start = (bf16[512,256]{0,1:T(8,128)(2,1)S(1)}, bf16[512,256]{0,1:T(8,128)(2,1)S(1)}, u32[]{:S(2)}, u32[]{:S(2)}) collective-permute-start(bf16[512,256]{0,1:T(8,128)(2,1)S(1)} %copy.23), channel_id=1, source_target_pairs={{0,3},{1,0},{2,1},{3,2},{4,7},{5,4},{6,5},{7,6},{8,11},{9,8},{10,9... | collective-permute-start | bytes 786440 | tf_op jit(solution)/shard_map/ppermute | solution.py:94
  94.5 24.1 %copy-start = (f32[256,2048]{1,0:T(8,128)S(1)}, f32[256,2048]{1,0:T(8,128)}, u32[]{:S(2)}) copy-start(f32[256,2048]{1,0:T(8,128)} %get-tuple-element.5) | copy-start | bytes 6291460
  100.6 17.4 %all-to-all-start.1 = ((f32[128,1,256]{2,1,0:T(1,128)}), f32[128,1,256]{2,1,0:T(1,128)S(1)}, u32[]{:S(2)}, u32[]{:S(2)}) async-start(f32[128,1,256]{2,1,0:T(1,128)} %broadcast_in_dim.9), calls=%async_computation.1 | async-start | bytes 262144 | tf_op jit(solution)/shard_map/all_to_all | solution.py:37
Sparse Core Ops, SparseCore 0:
  10.2 72.9 all-gather.2
